TPU v7x, 128 devices: a whole 4x4x4 slice. The times are simulated.
128 devices in a mesh: row: 8 (over z, core), col: 16 (over x, y).
Axes of the slice: x: 4, y: 4, z: 4, core: 2. Of those that a mesh axis runs over, the one named last changes fastest.
Arguments:
- spectra: bfloat16 [24576, 144, 128], P(('row', 'col')), may hold values from -30 to 30
- station_ids: int32 [24576], P(('row', 'col')), may hold values from 0 to 12287, as said below
- counts: int32 [128], P(('row', 'col')), may hold values from 0 to 192, as said below
Outputs:
- cross_spectra: bfloat16 [3, 2, 12288, 12288], P(None, None, 'row', 'col')
Inputs may be any that keep to these rules, and one draw needn't show every extreme that they name: `station_ids`: the live slots of all readers name every station exactly once; slots at or past a reader's count hold arbitrary station numbers and carry no data. The counts sum to 12288. Among the live slots of one reader, at most 2 name stations of one block h * 96 to h * 96 + 95, and that number is reached in every draw.
All inputs are finite; a program needn't handle non-finite values.
Results may differ from a plain program's by a relative error of at most 0.001.
Values may be sent and summed in bfloat16 or wider, within the bound.
A program may use at most 128 MiB of HBM per device.

v0:
```python
import functools
import math

import jax
import jax.numpy as jnp
from jax import lax
from jax.experimental import pallas as pl
from jax.experimental.pallas import tpu as pltpu
from jax.sharding import PartitionSpec as P

def whiten_kernel(ids_ref, counts_ref, x_ref, out_ref, used_ref):
    step = pl.program_id(0)
    group = x_ref.shape[0]
    homes = used_ref.shape[0]
    dummy = 2 * homes

    @pl.when(step == 0)
    def _():
        out_ref[...] = jnp.zeros_like(out_ref)
        def clear(i, c):
            used_ref[i] = 0
            return c
        lax.fori_loop(0, homes, clear, 0)

    x = x_ref[...]
    x = jnp.concatenate([x[:, :128].reshape(group * 128, 128), x[:, 128:].reshape(group * 16, 128)], axis=0)
    xf = x.astype(jnp.float32)
    energy = xf * xf
    high = energy.astype(jnp.bfloat16)
    low = (energy - high.astype(jnp.float32)).astype(jnp.bfloat16)
    q = lax.broadcasted_iota(jnp.int32, (8, 128), 0)
    lane = lax.broadcasted_iota(jnp.int32, (8, 128), 1)
    start = (q // 2) * 16
    inside = (q < 6) & ((lane & 63) >= start) & ((lane & 63) < start + 32)
    window = jnp.where(inside, 1.0, 0.0).astype(jnp.bfloat16)
    center = jnp.where((q < 6) & (lane == start + 16 + (q & 1) * 64), 1.0, 0.0).astype(jnp.bfloat16)
    contract = (((1,), (1,)), ((), ()))
    total = lax.dot_general(jnp.concatenate([window, window], axis=1), jnp.concatenate([high, low], axis=1),
                            contract, preferred_element_type=jnp.float32)
    values = lax.dot_general(center, x, contract, preferred_element_type=jnp.float32)
    white = values * lax.rsqrt(jnp.maximum(total * (1.0 / 32), 0.25))

    sub = lax.broadcasted_iota(jnp.int32, (8, 128), 0)
    chunk = lax.broadcasted_iota(jnp.int32, (8, 128), 1) // 16
    for part in range(group // 8):
        base = group * 128 + part * 128
        tail = white[:, base:base + 128]
        turned = jnp.zeros_like(tail)
        for d in range(8):
            piece = jnp.where(((chunk - sub) & 7) == d, tail, 0.0)
            if d:
                piece = pltpu.roll(pltpu.roll(piece, 128 - 16 * d, 1), d, 0)
            turned = turned + piece
        for k in range(8):
            j = part * 8 + k
            slot = step * group + j
            station = ids_ref[slot]
            home = (station * 43691) >> 22
            live = slot < counts_ref[0]
            seen = used_ref[home]
            used_ref[home] = jnp.where(live, seen + 1, seen)
            place = jnp.where(live, home * 2 + seen, dummy)
            mark = (station - home * 96 + 1).astype(jnp.float32)
            tile = jnp.where(sub < 6, white[:, j * 128:(j + 1) * 128],
                             jnp.where(sub == 6, jnp.broadcast_to(turned[k:k + 1], (8, 128)), mark))
            out_ref[place] = tile

def whiten_pack(spectra, ids, counts, homes, group=8):
    slots, segs, width = spectra.shape
    return pl.pallas_call(
        whiten_kernel,
        out_shape=jax.ShapeDtypeStruct((2 * homes + 8, 8, 128), jnp.float32),
        grid=(slots // group,),
        in_specs=[pl.BlockSpec(memory_space=pltpu.SMEM), pl.BlockSpec(memory_space=pltpu.SMEM),
                  pl.BlockSpec((group, segs, width), lambda i: (i, 0, 0))],
        out_specs=pl.BlockSpec((2 * homes + 8, 8, 128), lambda i: (0, 0, 0)),
        scratch_shapes=[pltpu.SMEM((homes,), jnp.int32)],
        name="whiten_pack",
    )(ids, counts, spectra)


MESH = pl.DeviceIdType.MESH
RING = 4
X, Y = 0, 1


def arrival(half, ox, oy, q):
    axes = (X, Y) if half == 0 else (Y, X)
    off = {X: ox, Y: oy}
    for axis in (axes[1], axes[0]):
        o = off[axis]
        if o:
            return (axis, 1) if o == 3 or (o == 2 and q == 0) else (axis, -1)
    return None


def row_plan():
    items = []
    for half in (0, 1):
        axes = (X, Y) if half == 0 else (Y, X)
        for ox in range(RING):
            for oy in range(RING):
                off = {X: ox, Y: oy}
                for q in (0, 1):
                    for level, axis in enumerate(axes):
                        if level == 0 and off[axes[1]]:
                            continue
                        o = off[axis]
                        for direction in (1, -1):
                            first = o == 0
                            onward = (o == 3 and direction == 1 and q == 0) or (o == 1 and direction == -1 and q == 1)
                            if first or onward:
                                depth = (2 if level == 0 else 0) + (1 if first else 0)
                                items.append(((half, ox, oy, q, axis, direction), depth))
    ready = {(half, 0, 0, q): 0 for half in (0, 1) for q in (0, 1)}
    busy = {}
    order = []
    left = list(items)
    time = 0
    while left:
        for link in ((X, 1), (X, -1), (Y, 1), (Y, -1)):
            best = None
            for entry in left:
                item, depth = entry
                if item[4:] == link and ready.get(item[:4], 99999) <= time:
                    key = (-depth, ready[item[:4]])
                    if best is None or key < best[0]:
                        best = (key, entry)
            if best is not None:
                entry = best[1]
                left.remove(entry)
                half, ox, oy, q, axis, direction = entry[0]
                order.append(entry[0])
                there = (half, (ox - direction) % RING if axis == X else ox,
                         (oy - direction) % RING if axis == Y else oy, q)
                assert arrival(*there) == (axis, direction) and there not in ready
                ready[there] = time + 2
        time += 1
    return order


def exchange_kernel(packed_ref, rows_ref, cols_ref, recv_ref, a2a_send, a2a_recv, own_sem,
                    row_send, row_recv, col_send, col_recv):
    r = lax.axis_index("row")
    c = lax.axis_index("col")
    nr, nc = lax.axis_size("row"), lax.axis_size("col")
    x, y = c // RING, c % RING
    n = nr * nc
    me = r * nc + c

    barrier = pltpu.get_barrier_semaphore()

    def peer(d):
        p = (me + d) % n
        return p, (p // nc, p % nc)

    def greet(d, carry):
        pl.semaphore_signal(barrier, inc=1, device_id=peer(d)[1], device_id_type=MESH)
        return carry
    lax.fori_loop(1, n, greet, 0)
    pl.semaphore_wait(barrier, n - 1)

    def slots(p):
        return pl.ds(pl.multiple_of(p * 16, 16), 16)

    def post(d, carry):
        p, where = peer(d)
        pltpu.make_async_remote_copy(packed_ref.at[slots(p)], recv_ref.at[slots(me)], a2a_send, a2a_recv,
                                     device_id=where, device_id_type=MESH).start()
        return carry
    lax.fori_loop(1, n, post, 0)
    mine = pltpu.make_async_copy(packed_ref.at[slots(me)], recv_ref.at[slots(me)], own_sem)
    mine.start()
    mine.wait()
    others = pl.ds(0, 16 * (n - 1))
    pltpu.make_async_copy(recv_ref.at[others], recv_ref.at[others], a2a_recv).wait()

    total = 2 * n
    sd = rows_ref.shape[2]
    mark = recv_ref[pl.ds(7, total, stride=8), :]
    lane = lax.broadcasted_iota(jnp.int32, mark.shape, 1)
    hit = jnp.where(mark == (lane + 1).astype(jnp.float32), 1.0, 0.0)
    pick = jnp.transpose(hit)[:sd].astype(jnp.bfloat16)
    for k in range(7):
        values = recv_ref[pl.ds(k, total, stride=8), :]
        high = values.astype(jnp.bfloat16)
        low = (values - high.astype(jnp.float32)).astype(jnp.bfloat16)
        placed = jnp.dot(pick, jnp.concatenate([high, low], axis=1),
                         preferred_element_type=jnp.float32).astype(jnp.bfloat16)
        for half in (0, 1):
            piece = placed[:, half * 128:(half + 1) * 128]
            rows_ref[half, c, :, k * 128:(k + 1) * 128] = piece
            cols_ref[half, r, :, k * 128:(k + 1) * 128] = piece

    part = sd // 2
    row_sem = {}

    def row_copy(item):
        half, ox, oy, q, axis, direction = item
        source = (x + ox) % RING * RING + (y + oy) % RING
        ref = rows_ref.at[half, source, pl.ds(q * part, part)]
        tx, ty = (x + direction) % RING, (y + direction) % RING
        target = (tx * RING + y) if axis == X else (x * RING + ty)
        there = (half, (ox - direction) % RING if axis == X else ox,
                 (oy - direction) % RING if axis == Y else oy, q)
        index = row_sem.setdefault(there, len(row_sem))
        return pltpu.make_async_remote_copy(ref, ref, row_send, row_recv.at[index],
                                            device_id=(r, target), device_id_type=MESH)

    def row_wait(half, ox, oy, q):
        source = (x + ox) % RING * RING + (y + oy) % RING
        ref = rows_ref.at[half, source, pl.ds(q * part, part)]
        pltpu.make_async_copy(ref, ref, row_recv.at[row_sem[(half, ox, oy, q)]]).wait()

    z, core = r // 2, r % 2
    col_sem = {}

    def col_copy(oz, q, link):
        source = (z + oz) % RING * 2 + core
        ref = cols_ref.at[:, source, pl.ds(q * part, part)]
        if link == 0:
            target = z * 2 + (1 - core)
            there = ("core", oz, q)
        else:
            target = (z + link) % RING * 2 + core
            there = ("z", (oz - link) % RING, q)
        index = col_sem.setdefault(there, len(col_sem))
        return pltpu.make_async_remote_copy(ref, ref, col_send, col_recv.at[index],
                                            device_id=(target, c), device_id_type=MESH)

    def col_wait(kind, oz, q):
        source = (z + oz) % RING * 2 + (core if kind == "z" else 1 - core)
        ref = cols_ref.at[:, source, pl.ds(q * part, part)]
        pltpu.make_async_copy(ref, ref, col_recv.at[col_sem[(kind, oz, q)]]).wait()

    plan = row_plan()
    first = [i for i in plan if i[1] == 0 and i[2] == 0]
    for item in plan:
        row_sem.setdefault((item[0], (item[1] - item[5]) % RING if item[4] == X else item[1],
                            (item[2] - item[5]) % RING if item[4] == Y else item[2], item[3]), len(row_sem))
    for q in (0, 1):
        col_copy(0, q, 1).start()
        col_copy(0, q, -1).start()
    for item in first:
        row_copy(item).start()
    for q in (0, 1):
        col_copy(0, q, 0).start()

    col_steps = [
        ("z", 3, 0, (1, 0)), ("z", 1, 1, (-1, 0)), ("z", 3, 1, (0,)), ("z", 1, 0, (0,)),
        ("z", 2, 0, (0,)), ("z", 2, 1, (0,)),
    ]
    waited = set()
    rest = [i for i in plan if i not in first]
    for number, item in enumerate(rest):
        if number % 4 == 3 and col_steps:
            kind, oz, q, links = col_steps.pop(0)
            col_wait(kind, oz, q)
            for link in links:
                col_copy(oz, q, link).start()
        chunk = item[:4]
        if chunk not in waited:
            row_wait(*chunk)
            waited.add(chunk)
        row_copy(item).start()
    for oz in range(RING):
        for q in (0, 1):
            col_wait("core", oz, q)
    for chunk in row_sem:
        if chunk not in waited:
            row_wait(*chunk)
    sent = packed_ref.at[others]
    pltpu.make_async_copy(sent, sent, a2a_send).wait()
    sent = rows_ref.at[:, pl.ds(0, nc - 1)]
    pltpu.make_async_copy(sent, sent, row_send).wait()
    sent = cols_ref.at[:, pl.ds(0, nr - 1)]
    pltpu.make_async_copy(sent, sent, col_send).wait()


def exchange(packed, nr, nc, sd):
    n = nr * nc
    dma = pltpu.SemaphoreType.DMA
    return pl.pallas_call(
        exchange_kernel,
        out_shape=(jax.ShapeDtypeStruct((2, nc, sd, 896), jnp.bfloat16),
                   jax.ShapeDtypeStruct((2, nr, sd, 896), jnp.bfloat16)),
        in_specs=[pl.BlockSpec(memory_space=pltpu.VMEM)],
        out_specs=(pl.BlockSpec(memory_space=pltpu.VMEM), pl.BlockSpec(memory_space=pltpu.VMEM)),
        scratch_shapes=[pltpu.VMEM((16 * n, 128), jnp.float32), dma, dma, dma,
                        dma, dma((60,)), dma, dma((14,))],
        compiler_params=pltpu.CompilerParams(collective_id=0, has_side_effects=True),
        name="exchange",
    )(packed)


def spread_tail(first, second, third, shift):
    lane = lax.broadcasted_iota(jnp.int32, first.shape, 1)
    out = jnp.where(lane < 32, pltpu.roll(first, (128 - shift) % 128, 1), 0.0)
    out = jnp.where((lane >= 32) & (lane < 64), pltpu.roll(second, (160 - shift) % 128, 1), out)
    return jnp.where((lane >= 64) & (lane < 96), pltpu.roll(third, (192 - shift) % 128, 1), out)

def prepare(cols_ref, rhs_ref):
    blocks, sd = cols_ref.shape[1], cols_ref.shape[2]
    n = blocks * sd
    lane = lax.broadcasted_iota(jnp.int32, (sd, 128), 1)
    for b in range(blocks):
        h = cols_ref[0, b]
        l = cols_ref[1, b]
        ht = h[:, 768:].astype(jnp.float32)
        lt = l[:, 768:].astype(jnp.float32)
        for f in range(3):
            hr, hi = h[:, 256 * f:256 * f + 128], h[:, 256 * f + 128:256 * f + 256]
            lr, li = l[:, 256 * f:256 * f + 128], l[:, 256 * f + 128:256 * f + 256]
            t = spread_tail(ht, lt, ht, 32 * f)
            u = jnp.where((lane & 16) == 0, -pltpu.roll(t, 112, 1), pltpu.roll(t, 16, 1))
            rhs_ref[f, b * sd:(b + 1) * sd] = jnp.concatenate([hr, hi, lr, li, hr, hi, t.astype(jnp.bfloat16)], axis=1)
            rhs_ref[f, n + b * sd:n + (b + 1) * sd] = jnp.concatenate([-hi, hr, -li, lr, -hi, hr, u.astype(jnp.bfloat16)], axis=1)

def pair_kernel(norm, cols_ref, rows_ref, out_ref, rhs_ref):
    @pl.when((pl.program_id(0) == 0))
    def _():
        prepare(cols_ref, rhs_ref)
    gb, sd = rows_ref.shape[1], rows_ref.shape[2]
    n = rhs_ref.shape[1] // 2
    h = rows_ref[0].reshape(gb * sd, -1)
    l = rows_ref[1].reshape(gb * sd, -1)
    ht = h[:, 768:].astype(jnp.float32)
    lt = l[:, 768:].astype(jnp.float32)
    for f in range(3):
        t = spread_tail(ht, ht, lt, 32 * f).astype(jnp.bfloat16)
        hm = h[:, 256 * f:256 * f + 256]
        lhs = jnp.concatenate([hm, hm, l[:, 256 * f:256 * f + 256], t], axis=1)
        p = lax.dot_general(lhs, rhs_ref[f], (((1,), (1,)), ((), ())), preferred_element_type=jnp.float32)
        p = (p * norm).astype(jnp.bfloat16)
        out_ref[f, 0] = p[:, :n]
        out_ref[f, 1] = p[:, n:]

def pair_products(rows, cols, norm, gb):
    _, nb, sd, width = rows.shape
    cb = cols.shape[1]
    n = cb * sd
    return pl.pallas_call(
        functools.partial(pair_kernel, norm),
        out_shape=jax.ShapeDtypeStruct((3, 2, nb * sd, n), jnp.bfloat16),
        grid=(nb // gb,),
        in_specs=[pl.BlockSpec((2, cb, sd, width), lambda i: (0, 0, 0, 0), pipeline_mode=pl.Buffered(1)),
                  pl.BlockSpec((2, gb, sd, width), lambda i: (0, i, 0, 0))],
        out_specs=pl.BlockSpec((3, 2, gb * sd, n), lambda i: (0, 0, i, 0)),
        scratch_shapes=[pltpu.VMEM((3, 2 * n, width), jnp.bfloat16)],
        name="pair_products",
    )(cols, rows)


def shards(spectra, station_ids, counts):
    row_count = lax.axis_size("row")
    column_count = lax.axis_size("col")
    readers = row_count * column_count
    slots, segments, _ = spectra.shape
    home_rows = slots // 2
    packed = whiten_pack(spectra, station_ids, counts, readers, group=48)
    packed = packed.reshape(-1, 128)
    rows, cols = exchange(packed, row_count, column_count, home_rows)
    return pair_products(rows, cols, 1.0 / math.sqrt(segments), 4)


def solution(mesh):
    in_specs = (P(("row", "col"), None, None), P(("row", "col")), P(("row", "col")))
    out_specs = P(None, None, "row", "col")
    return jax.shard_map(shards, mesh=mesh, in_specs=in_specs, out_specs=out_specs, check_vma=False)
```

profile of v0, /device:TPU:1, one launch (start us, length us, event | category | flops | bytes accessed | tf_op | source)
XLA Modules:
  0.0 95.5 jit_solution(10025593668554843404)
XLA Ops:
  0.7 10.2 %whiten_pack.1 = f32[264,8,128]{2,1,0:T(8,128)} custom-call(s32[192]{0:T(256)} %ids_ref.1, s32[1]{0:T(128)S(6)} %copy.4.counts_ref, bf16[192,144,128]{2,1,0:T(8,128)(2,1)} %x_ref.1), custom_call_target="tpu_custom_call" | custom-call | tf_op jit(solution)/shard_map/whiten_pack/pallas_call | solution.py:70
  10.8 62.8 %exchange.1 = (bf16[2,16,96,896]{3,2,1,0:T(8,128)(2,1)}, bf16[2,8,96,896]{3,2,1,0:T(8,128)(2,1)}) custom-call(f32[2112,128]{1,0:T(8,128)} %bitcast.1), custom_call_target="tpu_custom_call" | custom-call | tf_op jit(solution)/shard_map/exchange/pallas_call | solution.py:283
  73.6 21.9 %pair_products.1 = bf16[3,2,1536,768]{3,2,1,0:T(8,128)(2,1)} custom-call(bf16[2,8,96,896]{3,2,1,0:T(8,128)(2,1)} %get-tuple-element.7.cols_ref, bf16[2,16,96,896]{3,2,1,0:T(8,128)(2,1)} %get-tuple-element.8.rows_ref), custom_call_target="tpu_custom_call" | custom-call | tf_op jit(solution)/shard_map/pair_products/pallas_call | solution.py:342
where the time goes:
time: 95.7 us; the launch traced here: 95.5 us
  Pallas kernels  94.9 us (99%)
    pallas_call x1, Pallas kernels, exchange(): pl.pallas_call(exchange_kernel, out_shape=(jax.ShapeDtypeStruct((2, nc, s...  62.8 us
    pallas_call x1, Pallas kernels, pair_products(): pl.pallas_call(functools.partial(pair_kernel, norm), out_shape=jax.ShapeD...  21.9 us
    pallas_call x1, Pallas kernels, whiten_pack(): pl.pallas_call(whiten_kernel, out_shape=jax.ShapeDtypeStruct((2 * homes +...  10.2 us

commit v1 on v0

--- a/solution.py
+++ b/solution.py
@@ -9,12 +9,12 @@
 from jax.sharding import PartitionSpec as P
 
 def whiten_kernel(ids_ref, counts_ref, x_ref, out_ref, used_ref):
-    step = pl.program_id(0)
+    first = pl.program_id(0) == 0
+    step = pl.num_programs(0) - 1 - pl.program_id(0)
     group = x_ref.shape[0]
     homes = used_ref.shape[0]
-    dummy = 2 * homes
-
-    @pl.when(step == 0)
+
+    @pl.when(first)
     def _():
         out_ref[...] = jnp.zeros_like(out_ref)
         def clear(i, c):
@@ -42,7 +42,7 @@
 
     sub = lax.broadcasted_iota(jnp.int32, (8, 128), 0)
     chunk = lax.broadcasted_iota(jnp.int32, (8, 128), 1) // 16
-    for part in range(group // 8):
+    for part in reversed(range(group // 8)):
         base = group * 128 + part * 128
         tail = white[:, base:base + 128]
         turned = jnp.zeros_like(tail)
@@ -51,7 +51,7 @@
             if d:
                 piece = pltpu.roll(pltpu.roll(piece, 128 - 16 * d, 1), d, 0)
             turned = turned + piece
-        for k in range(8):
+        for k in reversed(range(8)):
             j = part * 8 + k
             slot = step * group + j
             station = ids_ref[slot]
@@ -59,22 +59,23 @@
             live = slot < counts_ref[0]
             seen = used_ref[home]
             used_ref[home] = jnp.where(live, seen + 1, seen)
-            place = jnp.where(live, home * 2 + seen, dummy)
+            place = jnp.where(live, seen * homes + home, 0)
             mark = (station - home * 96 + 1).astype(jnp.float32)
             tile = jnp.where(sub < 6, white[:, j * 128:(j + 1) * 128],
                              jnp.where(sub == 6, jnp.broadcast_to(turned[k:k + 1], (8, 128)), mark))
-            out_ref[place] = tile
+            out_ref[place] = jnp.where(live, tile, 0.0)
 
 def whiten_pack(spectra, ids, counts, homes, group=8):
     slots, segs, width = spectra.shape
     return pl.pallas_call(
         whiten_kernel,
-        out_shape=jax.ShapeDtypeStruct((2 * homes + 8, 8, 128), jnp.float32),
+        out_shape=jax.ShapeDtypeStruct((2 * homes, 8, 128), jnp.float32),
         grid=(slots // group,),
         in_specs=[pl.BlockSpec(memory_space=pltpu.SMEM), pl.BlockSpec(memory_space=pltpu.SMEM),
-                  pl.BlockSpec((group, segs, width), lambda i: (i, 0, 0))],
-        out_specs=pl.BlockSpec((2 * homes + 8, 8, 128), lambda i: (0, 0, 0)),
+                  pl.BlockSpec((group, segs, width), lambda i: (slots // group - 1 - i, 0, 0))],
+        out_specs=pl.BlockSpec((2 * homes, 8, 128), lambda i: (0, 0, 0)),
         scratch_shapes=[pltpu.SMEM((homes,), jnp.int32)],
+        compiler_params=pltpu.CompilerParams(vmem_limit_bytes=60 * 2**20),
         name="whiten_pack",
     )(ids, counts, spectra)
 
@@ -139,50 +140,64 @@
     return order
 
 
-def exchange_kernel(packed_ref, rows_ref, cols_ref, recv_ref, a2a_send, a2a_recv, own_sem,
+def exchange_kernel(packed_ref, rows_ref, cols_ref, mid0_ref, mid1_ref, recv0_ref, recv1_ref, own_sem, hop_send, hop_recv,
                     row_send, row_recv, col_send, col_recv):
     r = lax.axis_index("row")
     c = lax.axis_index("col")
     nr, nc = lax.axis_size("row"), lax.axis_size("col")
     x, y = c // RING, c % RING
-    n = nr * nc
-    me = r * nc + c
 
     barrier = pltpu.get_barrier_semaphore()
-
-    def peer(d):
-        p = (me + d) % n
-        return p, (p // nc, p % nc)
-
-    def greet(d, carry):
-        pl.semaphore_signal(barrier, inc=1, device_id=peer(d)[1], device_id_type=MESH)
-        return carry
-    lax.fori_loop(1, n, greet, 0)
-    pl.semaphore_wait(barrier, n - 1)
-
-    def slots(p):
-        return pl.ds(pl.multiple_of(p * 16, 16), 16)
-
-    def post(d, carry):
-        p, where = peer(d)
-        pltpu.make_async_remote_copy(packed_ref.at[slots(p)], recv_ref.at[slots(me)], a2a_send, a2a_recv,
+    row_peers = [(r + d) % nr for d in range(1, nr)]
+    col_peers = [(c + d) % nc for d in range(1, nc)]
+    for p in row_peers:
+        pl.semaphore_signal(barrier, inc=1, device_id=(p, c), device_id_type=MESH)
+    for p in col_peers:
+        pl.semaphore_signal(barrier, inc=1, device_id=(r, p), device_id_type=MESH)
+    pl.semaphore_wait(barrier, nr + nc - 2)
+
+    def send(source, target, where, k):
+        pltpu.make_async_remote_copy(source, target, hop_send.at[k], hop_recv.at[k],
                                      device_id=where, device_id_type=MESH).start()
-        return carry
-    lax.fori_loop(1, n, post, 0)
-    mine = pltpu.make_async_copy(packed_ref.at[slots(me)], recv_ref.at[slots(me)], own_sem)
-    mine.start()
-    mine.wait()
-    others = pl.ds(0, 16 * (n - 1))
-    pltpu.make_async_copy(recv_ref.at[others], recv_ref.at[others], a2a_recv).wait()
-
-    total = 2 * n
+
+    def keep(source, target, k):
+        pltpu.make_async_copy(source, target, own_sem.at[k]).start()
+
+    def arrive(ref, count, local, k):
+        others = ref.at[pl.ds(0, count)]
+        pltpu.make_async_copy(others, others, hop_recv.at[k]).wait()
+        pltpu.make_async_copy(local, local, own_sem.at[k]).wait()
+
+    for p in col_peers:
+        send(packed_ref.at[1, :, p], mid1_ref.at[c], (r, p), 1)
+    for p in row_peers:
+        send(packed_ref.at[0, p], mid0_ref.at[r], (p, c), 0)
+    keep(packed_ref.at[0, r], mid0_ref.at[r], 0)
+    keep(packed_ref.at[1, :, c], mid1_ref.at[c], 1)
+    arrive(mid0_ref, nr - 1, mid0_ref.at[r], 0)
+    for p in col_peers:
+        send(mid0_ref.at[:, p], recv0_ref.at[c], (r, p), 2)
+    keep(mid0_ref.at[:, c], recv0_ref.at[c], 2)
+    arrive(mid1_ref, nc - 1, mid1_ref.at[c], 1)
+    for p in row_peers:
+        send(mid1_ref.at[:, p], recv1_ref.at[r], (p, c), 3)
+    keep(mid1_ref.at[:, r], recv1_ref.at[r], 3)
+    arrive(recv0_ref, nc - 1, recv0_ref.at[c], 2)
+    arrive(recv1_ref, nr - 1, recv1_ref.at[r], 3)
+
+    half_slots = nr * nc
     sd = rows_ref.shape[2]
-    mark = recv_ref[pl.ds(7, total, stride=8), :]
+    flat = [ref.reshape(half_slots * 8, 128) for ref in (recv0_ref, recv1_ref)]
+
+    def plane(k):
+        return jnp.concatenate([ref[pl.ds(k, half_slots, stride=8), :] for ref in flat], axis=0)
+
+    mark = plane(7)
     lane = lax.broadcasted_iota(jnp.int32, mark.shape, 1)
     hit = jnp.where(mark == (lane + 1).astype(jnp.float32), 1.0, 0.0)
     pick = jnp.transpose(hit)[:sd].astype(jnp.bfloat16)
     for k in range(7):
-        values = recv_ref[pl.ds(k, total, stride=8), :]
+        values = plane(k)
         high = values.astype(jnp.bfloat16)
         low = (values - high.astype(jnp.float32)).astype(jnp.bfloat16)
         placed = jnp.dot(pick, jnp.concatenate([high, low], axis=1),
@@ -269,8 +284,9 @@
     for chunk in row_sem:
         if chunk not in waited:
             row_wait(*chunk)
-    sent = packed_ref.at[others]
-    pltpu.make_async_copy(sent, sent, a2a_send).wait()
+    for k, (ref, count) in enumerate([(mid0_ref, nr), (mid1_ref, nc), (recv0_ref, nc), (recv1_ref, nr)]):
+        sent = ref.at[pl.ds(0, count - 1)]
+        pltpu.make_async_copy(sent, sent, hop_send.at[k]).wait()
     sent = rows_ref.at[:, pl.ds(0, nc - 1)]
     pltpu.make_async_copy(sent, sent, row_send).wait()
     sent = cols_ref.at[:, pl.ds(0, nr - 1)]
@@ -278,7 +294,6 @@
 
 
 def exchange(packed, nr, nc, sd):
-    n = nr * nc
     dma = pltpu.SemaphoreType.DMA
     return pl.pallas_call(
         exchange_kernel,
@@ -286,9 +301,10 @@
                    jax.ShapeDtypeStruct((2, nr, sd, 896), jnp.bfloat16)),
         in_specs=[pl.BlockSpec(memory_space=pltpu.VMEM)],
         out_specs=(pl.BlockSpec(memory_space=pltpu.VMEM), pl.BlockSpec(memory_space=pltpu.VMEM)),
-        scratch_shapes=[pltpu.VMEM((16 * n, 128), jnp.float32), dma, dma, dma,
-                        dma, dma((60,)), dma, dma((14,))],
-        compiler_params=pltpu.CompilerParams(collective_id=0, has_side_effects=True),
+        scratch_shapes=[pltpu.VMEM((nr, nc, 8, 128), jnp.float32), pltpu.VMEM((nc, nr, 8, 128), jnp.float32),
+                        pltpu.VMEM((nc, nr, 8, 128), jnp.float32), pltpu.VMEM((nr, nc, 8, 128), jnp.float32),
+                        dma((4,)), dma((4,)), dma((4,)), dma, dma((60,)), dma, dma((14,))],
+        compiler_params=pltpu.CompilerParams(collective_id=0, has_side_effects=True, vmem_limit_bytes=16 * 2**20),
         name="exchange",
     )(packed)
 
@@ -347,6 +363,7 @@
                   pl.BlockSpec((2, gb, sd, width), lambda i: (0, i, 0, 0))],
         out_specs=pl.BlockSpec((3, 2, gb * sd, n), lambda i: (0, 0, i, 0)),
         scratch_shapes=[pltpu.VMEM((3, 2 * n, width), jnp.bfloat16)],
+        compiler_params=pltpu.CompilerParams(vmem_limit_bytes=40 * 2**20),
         name="pair_products",
     )(cols, rows)
 
@@ -358,7 +375,7 @@
     slots, segments, _ = spectra.shape
     home_rows = slots // 2
     packed = whiten_pack(spectra, station_ids, counts, readers, group=48)
-    packed = packed.reshape(-1, 128)
+    packed = packed.reshape(2, row_count, column_count, 8, 128)
     rows, cols = exchange(packed, row_count, column_count, home_rows)
     return pair_products(rows, cols, 1.0 / math.sqrt(segments), 4)
 

time: 95.7 us -> 89.5 us (0.935)
  Pallas kernels: 94.9 us -> 87.5 us
  local copies, waits for them, and re-layouts: 0 us -> 1.22 us
    pallas_call x1, Pallas kernels: 62.8 us -> 57 us  [exchange(): pl.pallas_call(exchange_kernel, out_shape=(jax.ShapeDtypeStruct((2, nc, s...]
    pallas_call x1, Pallas kernels: 21.9 us -> 20.1 us  [pair_products(): pl.pallas_call(functools.partial(pair_kernel, norm), out_shape=jax.ShapeD...]
    unnamed x0 -> x2, local copies, waits for them, and re-layouts: none -> 1.22 us
where the time goes in v1:
time: 89.5 us; the launch traced here: 89.4 us
  Pallas kernels  87.5 us (98%)
  local copies, waits for them, and re-layouts  1.22 us (1%)
    pallas_call x1, Pallas kernels, exchange(): pl.pallas_call(exchange_kernel, out_shape=(jax.ShapeDtypeStruct((2, nc, s...  57 us
    pallas_call x1, Pallas kernels, pair_products(): pl.pallas_call(functools.partial(pair_kernel, norm), out_shape=jax.ShapeD...  20.1 us
    pallas_call x1, Pallas kernels, whiten_pack(): pl.pallas_call(whiten_kernel, out_shape=jax.ShapeDtypeStruct((2 * homes,...  10.4 us

profile of v1, /device:TPU:1, one launch (start us, length us, event | category | flops | bytes accessed | tf_op | source)
XLA Modules:
  0.0 89.4 jit_solution(17499654422209008439)
XLA Ops:
  0.7 10.4 %whiten_pack.1 = f32[256,8,128]{2,1,0:T(8,128)} custom-call(s32[192]{0:T(256)} %ids_ref.1, s32[1]{0:T(128)S(6)} %copy.4.counts_ref, bf16[192,144,128]{2,1,0:T(8,128)(2,1)} %x_ref.1), custom_call_target="tpu_custom_call" | custom-call | tf_op jit(solution)/shard_map/whiten_pack/pallas_call | solution.py:70
  11.1 0.0 copy-start
  11.1 1.2 %copy-done = f32[256,8,128]{2,1,0:T(8,128)S(1)} copy-done((f32[256,8,128]{2,1,0:T(8,128)S(1)}, f32[256,8,128]{2,1,0:T(8,128)}, u32[]{:S(2)}) %copy-start) | copy-done | bytes 1048600
  12.3 57.0 %exchange.1 = (bf16[2,16,96,896]{3,2,1,0:T(8,128)(2,1)S(1)}, bf16[2,8,96,896]{3,2,1,0:T(8,128)(2,1)S(1)}) custom-call(f32[2,8,16,8,128]{4,3,2,1,0:T(8,128)S(1)} %bitcast.1), custom_call_target="tpu_custom_call" | custom-call | tf_op jit(solution)/shard_map/exchange/pallas_call | solution.py:298
  69.3 20.1 %pair_products.1 = bf16[3,2,1536,768]{3,2,1,0:T(8,128)(2,1)} custom-call(bf16[2,8,96,896]{3,2,1,0:T(8,128)(2,1)S(1)} %get-tuple-element.7.cols_ref, bf16[2,16,96,896]{3,2,1,0:T(8,128)(2,1)S(1)} %get-tuple-element.8.rows_ref), custom_call_target="tpu_custom_call" | custom-call | tf_op jit(solution)/shard_map/pair_products/pallas_call | solution.py:358
Async XLA Ops:
  11.1 1.2 %copy-start = (f32[256,8,128]{2,1,0:T(8,128)S(1)}, f32[256,8,128]{2,1,0:T(8,128)}, u32[]{:S(2)}) copy-start(f32[256,8,128]{2,1,0:T(8,128)} %whiten_pack.1) | copy-start | bytes 3145732

commit v2 on v1

--- a/solution.py
+++ b/solution.py
@@ -96,7 +96,7 @@
 
 
 def row_plan():
-    items = []
+    left = []
     for half in (0, 1):
         axes = (X, Y) if half == 0 else (Y, X)
         for ox in range(RING):
@@ -108,39 +108,47 @@
                             continue
                         o = off[axis]
                         for direction in (1, -1):
-                            first = o == 0
                             onward = (o == 3 and direction == 1 and q == 0) or (o == 1 and direction == -1 and q == 1)
-                            if first or onward:
-                                depth = (2 if level == 0 else 0) + (1 if first else 0)
-                                items.append(((half, ox, oy, q, axis, direction), depth))
+                            if o == 0 or onward:
+                                left.append((level, (half, ox, oy, q, axis, direction)))
     ready = {(half, 0, 0, q): 0 for half in (0, 1) for q in (0, 1)}
-    busy = {}
     order = []
-    left = list(items)
     time = 0
     while left:
         for link in ((X, 1), (X, -1), (Y, 1), (Y, -1)):
-            best = None
-            for entry in left:
-                item, depth = entry
-                if item[4:] == link and ready.get(item[:4], 99999) <= time:
-                    key = (-depth, ready[item[:4]])
-                    if best is None or key < best[0]:
-                        best = (key, entry)
-            if best is not None:
-                entry = best[1]
+            able = [e for e in left if e[1][4:] == link and ready.get(e[1][:4], time + 1) <= time]
+            if able:
+                entry = min(able, key=lambda e: (ready[e[1][:4]], e[0]))
                 left.remove(entry)
-                half, ox, oy, q, axis, direction = entry[0]
-                order.append(entry[0])
-                there = (half, (ox - direction) % RING if axis == X else ox,
-                         (oy - direction) % RING if axis == Y else oy, q)
-                assert arrival(*there) == (axis, direction) and there not in ready
+                order.append((time, entry[1]))
+                there = beyond(entry[1])
+                assert arrival(*there) == link and there not in ready
                 ready[there] = time + 2
         time += 1
-    return order
-
-
-def exchange_kernel(packed_ref, rows_ref, cols_ref, mid0_ref, mid1_ref, recv0_ref, recv1_ref, own_sem, hop_send, hop_recv,
+    whole = {}
+    for (half, ox, oy, q), when in ready.items():
+        whole[(ox, oy)] = max(whole.get((ox, oy), 0), when)
+    return order, sorted(whole.items(), key=lambda e: (e[1], e[0]))
+
+
+def beyond(item):
+    half, ox, oy, q, axis, direction = item
+    return (half, (ox - direction) % RING if axis == X else ox, (oy - direction) % RING if axis == Y else oy, q)
+
+
+GROUPS = (4, 4, 3)
+
+
+def block_groups():
+    blocks = [offset for offset, when in row_plan()[1]]
+    early = []
+    for size in GROUPS:
+        early.append(blocks[:size])
+        blocks = blocks[size:]
+    return early, blocks
+
+
+def exchange_kernel(norm, packed_ref, rows_ref, rhs_ref, part_ref, cols_ref, mid0_ref, mid1_ref, recv0_ref, recv1_ref, own_sem, hop_send, hop_recv,
                     row_send, row_recv, col_send, col_recv):
     r = lax.axis_index("row")
     c = lax.axis_index("col")
@@ -216,9 +224,7 @@
         ref = rows_ref.at[half, source, pl.ds(q * part, part)]
         tx, ty = (x + direction) % RING, (y + direction) % RING
         target = (tx * RING + y) if axis == X else (x * RING + ty)
-        there = (half, (ox - direction) % RING if axis == X else ox,
-                 (oy - direction) % RING if axis == Y else oy, q)
-        index = row_sem.setdefault(there, len(row_sem))
+        index = row_sem[beyond(item)]
         return pltpu.make_async_remote_copy(ref, ref, row_send, row_recv.at[index],
                                             device_id=(r, target), device_id_type=MESH)
 
@@ -248,42 +254,68 @@
         ref = cols_ref.at[:, source, pl.ds(q * part, part)]
         pltpu.make_async_copy(ref, ref, col_recv.at[col_sem[(kind, oz, q)]]).wait()
 
-    plan = row_plan()
-    first = [i for i in plan if i[1] == 0 and i[2] == 0]
-    for item in plan:
-        row_sem.setdefault((item[0], (item[1] - item[5]) % RING if item[4] == X else item[1],
-                            (item[2] - item[5]) % RING if item[4] == Y else item[2], item[3]), len(row_sem))
+    order, whole = row_plan()
+
+    def multiply(product):
+        _, group, position, f = product
+        for ox, oy in group:
+            for half in (0, 1):
+                for q in (0, 1):
+                    row_ready((half, ox, oy, q))
+        blocks = [(x + ox) % RING * RING + (y + oy) % RING for ox, oy in group]
+        real, imag = products_of(rows_ref, rhs_ref, blocks, f, norm)
+        for i in range(len(group)):
+            part_ref[position + i, f, 0] = real[i * sd:(i + 1) * sd]
+            part_ref[position + i, f, 1] = imag[i * sd:(i + 1) * sd]
+
+    for _, item in order:
+        row_sem.setdefault(beyond(item), len(row_sem))
+    waited = set()
+
+    def row_ready(chunk):
+        if chunk in row_sem and chunk not in waited:
+            row_wait(*chunk)
+            waited.add(chunk)
+
     for q in (0, 1):
-        col_copy(0, q, 1).start()
-        col_copy(0, q, -1).start()
-    for item in first:
-        row_copy(item).start()
-    for q in (0, 1):
-        col_copy(0, q, 0).start()
-
-    col_steps = [
-        ("z", 3, 0, (1, 0)), ("z", 1, 1, (-1, 0)), ("z", 3, 1, (0,)), ("z", 1, 0, (0,)),
-        ("z", 2, 0, (0,)), ("z", 2, 1, (0,)),
-    ]
-    waited = set()
-    rest = [i for i in plan if i not in first]
-    for number, item in enumerate(rest):
-        if number % 4 == 3 and col_steps:
-            kind, oz, q, links = col_steps.pop(0)
+        for link in (1, -1, 0):
+            col_copy(0, q, link).start()
+    col_steps = {3: [("z", 3, 0, (1, 0)), ("z", 1, 0, (0,))], 5: [("z", 1, 1, (-1, 0)), ("z", 3, 1, (0,))],
+                 7: [("z", 2, 0, (0,)), ("z", 2, 1, (0,))]}
+    col_jobs = {0: [("z", 0)], 1: [("core", 0)], 5: [("z", 3), ("z", 1)], 6: [("core", 3), ("core", 1)],
+                7: [("z", 2)], 8: [("core", 2)]}
+    early, _ = block_groups()
+    done_at = dict(whole)
+    products = []
+    position = 0
+    for group in early:
+        for f in range(3):
+            products.append((max(done_at[b] for b in group), group, position, f))
+        position += len(group)
+    last = max(t for t, _ in order)
+
+    for time in range(last + 1):
+        for step in col_steps.get(time, []):
+            kind, oz, q, links = step
             col_wait(kind, oz, q)
             for link in links:
                 col_copy(oz, q, link).start()
-        chunk = item[:4]
-        if chunk not in waited:
-            row_wait(*chunk)
-            waited.add(chunk)
-        row_copy(item).start()
-    for oz in range(RING):
-        for q in (0, 1):
-            col_wait("core", oz, q)
+        for when, item in order:
+            if when == time:
+                row_ready(item[:4])
+                row_copy(item).start()
+        for kind, oz in col_jobs.get(time, []):
+            if kind == "core":
+                col_wait(kind, oz, 0)
+                col_wait(kind, oz, 1)
+            source = (z + oz) % RING * 2 + (core if kind == "z" else 1 - core)
+            prepare(cols_ref[0, source], cols_ref[1, source], rhs_ref, pl.multiple_of(source * sd, 32), nr * sd)
+        if time >= 8 and products and products[0][0] <= time:
+            multiply(products.pop(0))
+    while products:
+        multiply(products.pop(0))
     for chunk in row_sem:
-        if chunk not in waited:
-            row_wait(*chunk)
+        row_ready(chunk)
     for k, (ref, count) in enumerate([(mid0_ref, nr), (mid1_ref, nc), (recv0_ref, nc), (recv1_ref, nr)]):
         sent = ref.at[pl.ds(0, count - 1)]
         pltpu.make_async_copy(sent, sent, hop_send.at[k]).wait()
@@ -293,18 +325,22 @@
     pltpu.make_async_copy(sent, sent, col_send).wait()
 
 
-def exchange(packed, nr, nc, sd):
+def exchange(packed, nr, nc, sd, norm):
     dma = pltpu.SemaphoreType.DMA
+    n = nr * sd
+    vmem = pl.BlockSpec(memory_space=pltpu.VMEM)
     return pl.pallas_call(
-        exchange_kernel,
+        functools.partial(exchange_kernel, norm),
         out_shape=(jax.ShapeDtypeStruct((2, nc, sd, 896), jnp.bfloat16),
-                   jax.ShapeDtypeStruct((2, nr, sd, 896), jnp.bfloat16)),
-        in_specs=[pl.BlockSpec(memory_space=pltpu.VMEM)],
-        out_specs=(pl.BlockSpec(memory_space=pltpu.VMEM), pl.BlockSpec(memory_space=pltpu.VMEM)),
-        scratch_shapes=[pltpu.VMEM((nr, nc, 8, 128), jnp.float32), pltpu.VMEM((nc, nr, 8, 128), jnp.float32),
+                   jax.ShapeDtypeStruct((3, 2 * n, 896), jnp.bfloat16),
+                   jax.ShapeDtypeStruct((sum(GROUPS), 3, 2, sd, n), jnp.bfloat16)),
+        in_specs=[pl.BlockSpec(memory_space=pltpu.HBM)],
+        out_specs=(vmem, vmem, vmem),
+        scratch_shapes=[pltpu.VMEM((2, nr, sd, 896), jnp.bfloat16),
+                        pltpu.VMEM((nr, nc, 8, 128), jnp.float32), pltpu.VMEM((nc, nr, 8, 128), jnp.float32),
                         pltpu.VMEM((nc, nr, 8, 128), jnp.float32), pltpu.VMEM((nr, nc, 8, 128), jnp.float32),
                         dma((4,)), dma((4,)), dma((4,)), dma, dma((60,)), dma, dma((14,))],
-        compiler_params=pltpu.CompilerParams(collective_id=0, has_side_effects=True, vmem_limit_bytes=16 * 2**20),
+        compiler_params=pltpu.CompilerParams(collective_id=0, has_side_effects=True, vmem_limit_bytes=24 * 2**20),
         name="exchange",
     )(packed)
 
@@ -315,57 +351,81 @@
     out = jnp.where((lane >= 32) & (lane < 64), pltpu.roll(second, (160 - shift) % 128, 1), out)
     return jnp.where((lane >= 64) & (lane < 96), pltpu.roll(third, (192 - shift) % 128, 1), out)
 
-def prepare(cols_ref, rhs_ref):
-    blocks, sd = cols_ref.shape[1], cols_ref.shape[2]
-    n = blocks * sd
+
+def prepare(h, l, rhs_ref, at, n):
+    sd = h.shape[0]
     lane = lax.broadcasted_iota(jnp.int32, (sd, 128), 1)
-    for b in range(blocks):
-        h = cols_ref[0, b]
-        l = cols_ref[1, b]
-        ht = h[:, 768:].astype(jnp.float32)
-        lt = l[:, 768:].astype(jnp.float32)
-        for f in range(3):
-            hr, hi = h[:, 256 * f:256 * f + 128], h[:, 256 * f + 128:256 * f + 256]
-            lr, li = l[:, 256 * f:256 * f + 128], l[:, 256 * f + 128:256 * f + 256]
-            t = spread_tail(ht, lt, ht, 32 * f)
-            u = jnp.where((lane & 16) == 0, -pltpu.roll(t, 112, 1), pltpu.roll(t, 16, 1))
-            rhs_ref[f, b * sd:(b + 1) * sd] = jnp.concatenate([hr, hi, lr, li, hr, hi, t.astype(jnp.bfloat16)], axis=1)
-            rhs_ref[f, n + b * sd:n + (b + 1) * sd] = jnp.concatenate([-hi, hr, -li, lr, -hi, hr, u.astype(jnp.bfloat16)], axis=1)
-
-def pair_kernel(norm, cols_ref, rows_ref, out_ref, rhs_ref):
-    @pl.when((pl.program_id(0) == 0))
-    def _():
-        prepare(cols_ref, rhs_ref)
-    gb, sd = rows_ref.shape[1], rows_ref.shape[2]
-    n = rhs_ref.shape[1] // 2
-    h = rows_ref[0].reshape(gb * sd, -1)
-    l = rows_ref[1].reshape(gb * sd, -1)
     ht = h[:, 768:].astype(jnp.float32)
     lt = l[:, 768:].astype(jnp.float32)
     for f in range(3):
-        t = spread_tail(ht, ht, lt, 32 * f).astype(jnp.bfloat16)
-        hm = h[:, 256 * f:256 * f + 256]
-        lhs = jnp.concatenate([hm, hm, l[:, 256 * f:256 * f + 256], t], axis=1)
-        p = lax.dot_general(lhs, rhs_ref[f], (((1,), (1,)), ((), ())), preferred_element_type=jnp.float32)
-        p = (p * norm).astype(jnp.bfloat16)
-        out_ref[f, 0] = p[:, :n]
-        out_ref[f, 1] = p[:, n:]
-
-def pair_products(rows, cols, norm, gb):
-    _, nb, sd, width = rows.shape
-    cb = cols.shape[1]
-    n = cb * sd
+        hr, hi = h[:, 256 * f:256 * f + 128], h[:, 256 * f + 128:256 * f + 256]
+        lr, li = l[:, 256 * f:256 * f + 128], l[:, 256 * f + 128:256 * f + 256]
+        t = spread_tail(ht, lt, ht, 32 * f)
+        u = jnp.where((lane & 16) == 0, -pltpu.roll(t, 112, 1), pltpu.roll(t, 16, 1))
+        rhs_ref[f, pl.ds(at, sd)] = jnp.concatenate([hr, hi, lr, li, hr, hi, t.astype(jnp.bfloat16)], axis=1)
+        rhs_ref[f, pl.ds(at + n, sd)] = jnp.concatenate([-hi, hr, -li, lr, -hi, hr, u.astype(jnp.bfloat16)], axis=1)
+
+
+def products_of(rows_ref, rhs_ref, blocks, f, norm):
+    n = rhs_ref.shape[1] // 2
+
+    def take(half, start, width):
+        return jnp.concatenate([rows_ref[half, b, :, start:start + width] for b in blocks], axis=0)
+    ht = take(0, 768, 128).astype(jnp.float32)
+    lt = take(1, 768, 128).astype(jnp.float32)
+    high = take(0, 256 * f, 256)
+    lhs = jnp.concatenate([high, high, take(1, 256 * f, 256), spread_tail(ht, ht, lt, 32 * f).astype(jnp.bfloat16)], axis=1)
+    p = lax.dot_general(lhs, rhs_ref[f], (((1,), (1,)), ((), ())), preferred_element_type=jnp.float32)
+    p = (p * norm).astype(jnp.bfloat16)
+    return p[:, :n], p[:, n:]
+
+
+def finish_kernel(norm, rows_ref, rhs_ref, part_ref, out_ref, rest_ref, part_sem, rest_sem):
+    c = lax.axis_index("col")
+    x, y = c // RING, c % RING
+    sd = rows_ref.shape[2]
+    early, late = block_groups()
+
+    def block(offset):
+        return (x + offset[0]) % RING * RING + (y + offset[1]) % RING
+
+    def rows_of(b):
+        return pl.ds(pl.multiple_of(b * sd, 32), sd)
+
+    place = [block(o) for group in early for o in group]
+    for i, b in enumerate(place):
+        pltpu.make_async_copy(part_ref.at[i], out_ref.at[:, :, rows_of(b)], part_sem.at[i]).start()
+    blocks = [block(o) for o in late]
+    for f in range(3):
+        real, imag = products_of(rows_ref, rhs_ref, blocks, f, norm)
+        rest_ref[f, 0] = real
+        rest_ref[f, 1] = imag
+        for i, b in enumerate(blocks):
+            pltpu.make_async_copy(rest_ref.at[f, :, pl.ds(i * sd, sd)], out_ref.at[f, :, rows_of(b)],
+                                  rest_sem.at[f, i]).start()
+    for i, b in enumerate(place):
+        pltpu.make_async_copy(part_ref.at[i], out_ref.at[:, :, rows_of(b)], part_sem.at[i]).wait()
+    for f in range(3):
+        for i, b in enumerate(blocks):
+            pltpu.make_async_copy(rest_ref.at[f, :, pl.ds(i * sd, sd)], out_ref.at[f, :, rows_of(b)],
+                                  rest_sem.at[f, i]).wait()
+
+
+def finish(rows, rhs, part, norm):
+    _, nc, sd, _ = rows.shape
+    n = rhs.shape[1] // 2
+    late = nc - part.shape[0]
+    dma = pltpu.SemaphoreType.DMA
+    vmem = pl.BlockSpec(memory_space=pltpu.VMEM)
     return pl.pallas_call(
-        functools.partial(pair_kernel, norm),
-        out_shape=jax.ShapeDtypeStruct((3, 2, nb * sd, n), jnp.bfloat16),
-        grid=(nb // gb,),
-        in_specs=[pl.BlockSpec((2, cb, sd, width), lambda i: (0, 0, 0, 0), pipeline_mode=pl.Buffered(1)),
-                  pl.BlockSpec((2, gb, sd, width), lambda i: (0, i, 0, 0))],
-        out_specs=pl.BlockSpec((3, 2, gb * sd, n), lambda i: (0, 0, i, 0)),
-        scratch_shapes=[pltpu.VMEM((3, 2 * n, width), jnp.bfloat16)],
-        compiler_params=pltpu.CompilerParams(vmem_limit_bytes=40 * 2**20),
-        name="pair_products",
-    )(cols, rows)
+        functools.partial(finish_kernel, norm),
+        out_shape=jax.ShapeDtypeStruct((3, 2, nc * sd, n), jnp.bfloat16),
+        in_specs=[vmem, vmem, vmem],
+        out_specs=pl.BlockSpec(memory_space=pl.ANY),
+        scratch_shapes=[pltpu.VMEM((3, 2, late * sd, n), jnp.bfloat16), dma((nc - late,)), dma((3, late))],
+        compiler_params=pltpu.CompilerParams(vmem_limit_bytes=24 * 2**20),
+        name="finish",
+    )(rows, rhs, part)
 
 
 def shards(spectra, station_ids, counts):
@@ -376,8 +436,9 @@
     home_rows = slots // 2
     packed = whiten_pack(spectra, station_ids, counts, readers, group=48)
     packed = packed.reshape(2, row_count, column_count, 8, 128)
-    rows, cols = exchange(packed, row_count, column_count, home_rows)
-    return pair_products(rows, cols, 1.0 / math.sqrt(segments), 4)
+    norm = 1.0 / math.sqrt(segments)
+    rows, rhs, part = exchange(packed, row_count, column_count, home_rows, norm)
+    return finish(rows, rhs, part, norm)
 
 
 def solution(mesh):

time: 89.5 us -> 77.5 us (0.87)
  Pallas kernels: 87.5 us -> 75.5 us
    pallas_call x2, Pallas kernels: 77.1 us -> 65.1 us  [the longest x1 57.8 us: exchange(): pl.pallas_call(functools.partial(exchange_kernel, norm), out_shape=(jax.S...]
where the time goes in v2:
time: 77.5 us; the launch traced here: 77.3 us
  Pallas kernels  75.5 us (97%)
  local copies, waits for them, and re-layouts  1.22 us (2%)
    pallas_call x1, Pallas kernels, exchange(): pl.pallas_call(functools.partial(exchange_kernel, norm), out_shape=(jax.S...  57.8 us
    pallas_call x1, Pallas kernels, whiten_pack(): pl.pallas_call(whiten_kernel, out_shape=jax.ShapeDtypeStruct((2 * homes,...  10.4 us
    pallas_call x1, Pallas kernels, finish(): pl.pallas_call(functools.partial(finish_kernel, norm), out_shape=jax.Shap...  7.21 us

profile of v2, /device:TPU:1, one launch (start us, length us, event | category | flops | bytes accessed | tf_op | source)
XLA Modules:
  0.0 77.3 jit_solution(2286700252847418550)
XLA Ops:
  0.7 10.4 %whiten_pack.1 = f32[256,8,128]{2,1,0:T(8,128)} custom-call(s32[192]{0:T(256)} %ids_ref.1, s32[1]{0:T(128)S(6)} %copy.4.counts_ref, bf16[192,144,128]{2,1,0:T(8,128)(2,1)} %x_ref.1), custom_call_target="tpu_custom_call" | custom-call | tf_op jit(solution)/shard_map/whiten_pack/pallas_call | solution.py:70
  11.1 0.0 copy-start
  11.1 1.2 %copy-done = f32[256,8,128]{2,1,0:T(8,128)S(1)} copy-done((f32[256,8,128]{2,1,0:T(8,128)S(1)}, f32[256,8,128]{2,1,0:T(8,128)}, u32[]{:S(2)}) %copy-start) | copy-done | bytes 1048600
  12.3 57.8 %exchange.1 = (bf16[2,16,96,896]{3,2,1,0:T(8,128)(2,1)S(1)}, bf16[3,1536,896]{2,1,0:T(8,128)(2,1)S(1)}, bf16[11,3,2,96,768]{4,3,2,1,0:T(8,128)(2,1)S(1)}) custom-call(f32[2,8,16,8,128]{4,3,2,1,0:T(8,128)S(1)} %bitcast.1), custom_call_target="tpu_custom_call" | custom-call | tf_op jit(solution)/shard_map/exchange/pallas_call | solution.py:332
  70.1 7.2 %finish.1 = bf16[3,2,1536,768]{3,2,1,0:T(8,128)(2,1)} custom-call(bf16[2,16,96,896]{3,2,1,0:T(8,128)(2,1)S(1)} %get-tuple-element.8.rows_ref, bf16[3,1536,896]{2,1,0:T(8,128)(2,1)S(1)} %get-tuple-element.9.rhs_ref, bf16[11,3,2,96,768]{4,3,2,1,0:T(8,128)(2,1)S(1)} %get-tuple-element.10.part_ref), custom_call_target="tpu_custom_call" | custom-call | tf_op jit(solution)/shard_map/finish/pallas_call | solution.py:420
Async XLA Ops:
  11.1 1.2 %copy-start = (f32[256,8,128]{2,1,0:T(8,128)S(1)}, f32[256,8,128]{2,1,0:T(8,128)}, u32[]{:S(2)}) copy-start(f32[256,8,128]{2,1,0:T(8,128)} %whiten_pack.1) | copy-start | bytes 3145732

commit v3 on v2

--- a/solution.py
+++ b/solution.py
@@ -136,7 +136,7 @@
     return (half, (ox - direction) % RING if axis == X else ox, (oy - direction) % RING if axis == Y else oy, q)
 
 
-GROUPS = (4, 4, 3)
+GROUPS = (4, 4, 3, 2)
 
 
 def block_groups():
@@ -171,27 +171,48 @@
     def keep(source, target, k):
         pltpu.make_async_copy(source, target, own_sem.at[k]).start()
 
-    def arrive(ref, count, local, k):
-        others = ref.at[pl.ds(0, count)]
+    z, core = r // 2, r % 2
+    y_high, parity = y // 2, y % 2
+
+    def columns(j):
+        return [((x + dx) % RING, (y + dy) % RING) for dx in range(RING) for dy in range(j, RING, 2) if dx or dy]
+
+    def rows_at(j):
+        return [((z + dz) % RING, (core + j) % 2) for dz in range(RING) if dz or j]
+
+    for j in (0, 1):
+        h0, h1 = (parity + j) % 2, (core + j) % 2
+        for px, py in columns(0) + columns(1):
+            send(packed_ref.at[1, :, h1, px, py // 2, py % 2], mid1_ref.at[c, :, h1], (r, px * RING + py), 2 + j)
+        for pz, pc in rows_at(0) + rows_at(1):
+            send(packed_ref.at[0, pz, pc, :, :, h0], mid0_ref.at[r, :, :, h0], (pz * 2 + pc, c), j)
+        keep(packed_ref.at[0, z, core, :, :, h0], mid0_ref.at[r, :, :, h0], j)
+        keep(packed_ref.at[1, :, h1, x, y_high, parity], mid1_ref.at[c, :, h1], 2 + j)
+
+    def arrive(others, local, k):
         pltpu.make_async_copy(others, others, hop_recv.at[k]).wait()
         pltpu.make_async_copy(local, local, own_sem.at[k]).wait()
 
-    for p in col_peers:
-        send(packed_ref.at[1, :, p], mid1_ref.at[c], (r, p), 1)
-    for p in row_peers:
-        send(packed_ref.at[0, p], mid0_ref.at[r], (p, c), 0)
-    keep(packed_ref.at[0, r], mid0_ref.at[r], 0)
-    keep(packed_ref.at[1, :, c], mid1_ref.at[c], 1)
-    arrive(mid0_ref, nr - 1, mid0_ref.at[r], 0)
-    for p in col_peers:
-        send(mid0_ref.at[:, p], recv0_ref.at[c], (r, p), 2)
-    keep(mid0_ref.at[:, c], recv0_ref.at[c], 2)
-    arrive(mid1_ref, nc - 1, mid1_ref.at[c], 1)
-    for p in row_peers:
-        send(mid1_ref.at[:, p], recv1_ref.at[r], (p, c), 3)
-    keep(mid1_ref.at[:, r], recv1_ref.at[r], 3)
-    arrive(recv0_ref, nc - 1, recv0_ref.at[c], 2)
-    arrive(recv1_ref, nr - 1, recv1_ref.at[r], 3)
+    sent = []
+    for j in (0, 1):
+        h0, h1 = (parity + j) % 2, (core + j) % 2
+        others = mid0_ref.at[pl.ds(0, nr - 1), :, :, h0]
+        sent.append((others, j))
+        arrive(others, mid0_ref.at[r, :, :, h0], j)
+        for px, py in columns(j):
+            send(mid0_ref.at[:, px, py // 2, h0], recv0_ref.at[c], (r, px * RING + py), 4)
+        others = mid1_ref.at[pl.ds(0, nc - 1), :, h1]
+        sent.append((others, 2 + j))
+        arrive(others, mid1_ref.at[c, :, h1], 2 + j)
+        for pz, pc in rows_at(j):
+            send(mid1_ref.at[:, pz, h1], recv1_ref.at[r], (pz * 2 + pc, c), 5)
+        if j == 0:
+            keep(mid0_ref.at[:, x, y_high, parity], recv0_ref.at[c], 4)
+            keep(mid1_ref.at[:, z, core], recv1_ref.at[r], 5)
+    for ref, count, local, k in ((recv0_ref, nc, c, 4), (recv1_ref, nr, r, 5)):
+        others = ref.at[pl.ds(0, count - 1)]
+        sent.append((others, k))
+        arrive(others, ref.at[local], k)
 
     half_slots = nr * nc
     sd = rows_ref.shape[2]
@@ -233,7 +254,6 @@
         ref = rows_ref.at[half, source, pl.ds(q * part, part)]
         pltpu.make_async_copy(ref, ref, row_recv.at[row_sem[(half, ox, oy, q)]]).wait()
 
-    z, core = r // 2, r % 2
     col_sem = {}
 
     def col_copy(oz, q, link):
@@ -316,9 +336,8 @@
         multiply(products.pop(0))
     for chunk in row_sem:
         row_ready(chunk)
-    for k, (ref, count) in enumerate([(mid0_ref, nr), (mid1_ref, nc), (recv0_ref, nc), (recv1_ref, nr)]):
-        sent = ref.at[pl.ds(0, count - 1)]
-        pltpu.make_async_copy(sent, sent, hop_send.at[k]).wait()
+    for ref, k in sent:
+        pltpu.make_async_copy(ref, ref, hop_send.at[k]).wait()
     sent = rows_ref.at[:, pl.ds(0, nc - 1)]
     pltpu.make_async_copy(sent, sent, row_send).wait()
     sent = cols_ref.at[:, pl.ds(0, nr - 1)]
@@ -337,9 +356,10 @@
         in_specs=[pl.BlockSpec(memory_space=pltpu.HBM)],
         out_specs=(vmem, vmem, vmem),
         scratch_shapes=[pltpu.VMEM((2, nr, sd, 896), jnp.bfloat16),
-                        pltpu.VMEM((nr, nc, 8, 128), jnp.float32), pltpu.VMEM((nc, nr, 8, 128), jnp.float32),
+                        pltpu.VMEM((nr, RING, 2, 2, 8, 128), jnp.float32),
+                        pltpu.VMEM((nc, RING, 2, 8, 128), jnp.float32),
                         pltpu.VMEM((nc, nr, 8, 128), jnp.float32), pltpu.VMEM((nr, nc, 8, 128), jnp.float32),
-                        dma((4,)), dma((4,)), dma((4,)), dma, dma((60,)), dma, dma((14,))],
+                        dma((6,)), dma((6,)), dma((6,)), dma, dma((60,)), dma, dma((14,))],
         compiler_params=pltpu.CompilerParams(collective_id=0, has_side_effects=True, vmem_limit_bytes=24 * 2**20),
         name="exchange",
     )(packed)
@@ -435,7 +455,7 @@
     slots, segments, _ = spectra.shape
     home_rows = slots // 2
     packed = whiten_pack(spectra, station_ids, counts, readers, group=48)
-    packed = packed.reshape(2, row_count, column_count, 8, 128)
+    packed = packed.reshape(2, RING, 2, RING, 2, 2, 8, 128)
     norm = 1.0 / math.sqrt(segments)
     rows, rhs, part = exchange(packed, row_count, column_count, home_rows, norm)
     return finish(rows, rhs, part, norm)

time: 77.5 us -> 74 us (0.955)
  Pallas kernels: 75.5 us -> 71.8 us
    pallas_call x1, Pallas kernels: 57.8 us -> 55 us  [exchange(): pl.pallas_call(functools.partial(exchange_kernel, norm), out_shape=(jax.S...]
    pallas_call x1, Pallas kernels: 7.21 us -> 6.38 us  [finish(): pl.pallas_call(functools.partial(finish_kernel, norm), out_shape=jax.Shap...]
where the time goes in v3:
time: 74 us; the launch traced here: 73.8 us
  Pallas kernels  71.8 us (97%)
  local copies, waits for them, and re-layouts  1.22 us (2%)
  between operations  0.82 us (1%)
    pallas_call x1, Pallas kernels, exchange(): pl.pallas_call(functools.partial(exchange_kernel, norm), out_shape=(jax.S...  55 us
    pallas_call x1, Pallas kernels, whiten_pack(): pl.pallas_call(whiten_kernel, out_shape=jax.ShapeDtypeStruct((2 * homes,...  10.4 us
    pallas_call x1, Pallas kernels, finish(): pl.pallas_call(functools.partial(finish_kernel, norm), out_shape=jax.Shap...  6.38 us

profile of v3, /device:TPU:1, one launch (start us, length us, event | category | flops | bytes accessed | tf_op | source)
XLA Modules:
  0.0 73.8 jit_solution(7038978841706151650)
XLA Ops:
  0.7 10.4 %whiten_pack.1 = f32[256,8,128]{2,1,0:T(8,128)} custom-call(s32[192]{0:T(256)} %ids_ref.1, s32[1]{0:T(128)S(6)} %copy.4.counts_ref, bf16[192,144,128]{2,1,0:T(8,128)(2,1)} %x_ref.1), custom_call_target="tpu_custom_call" | custom-call | tf_op jit(solution)/shard_map/whiten_pack/pallas_call | solution.py:70
  11.1 0.0 copy-start
  11.1 1.2 %copy-done = f32[256,8,128]{2,1,0:T(8,128)S(1)} copy-done((f32[256,8,128]{2,1,0:T(8,128)S(1)}, f32[256,8,128]{2,1,0:T(8,128)}, u32[]{:S(2)}) %copy-start) | copy-done | bytes 1048600
  12.3 55.0 %exchange.1 = (bf16[2,16,96,896]{3,2,1,0:T(8,128)(2,1)S(1)}, bf16[3,1536,896]{2,1,0:T(8,128)(2,1)S(1)}, bf16[13,3,2,96,768]{4,3,2,1,0:T(8,128)(2,1)S(1)}) custom-call(f32[2,4,2,4,2,2,8,128]{7,6,5,4,3,2,1,0:T(8,128)S(1)} %bitcast.1), custom_call_target="tpu_custom_call" | custom-call | tf_op jit(solution)/shard_map/exchange/pallas_call | solution.py:351
  67.3 6.4 %finish.1 = bf16[3,2,1536,768]{3,2,1,0:T(8,128)(2,1)} custom-call(bf16[2,16,96,896]{3,2,1,0:T(8,128)(2,1)S(1)} %get-tuple-element.8.rows_ref, bf16[3,1536,896]{2,1,0:T(8,128)(2,1)S(1)} %get-tuple-element.9.rhs_ref, bf16[13,3,2,96,768]{4,3,2,1,0:T(8,128)(2,1)S(1)} %get-tuple-element.10.part_ref), custom_call_target="tpu_custom_call" | custom-call | tf_op jit(solution)/shard_map/finish/pallas_call | solution.py:440
Async XLA Ops:
  11.1 1.2 %copy-start = (f32[256,8,128]{2,1,0:T(8,128)S(1)}, f32[256,8,128]{2,1,0:T(8,128)}, u32[]{:S(2)}) copy-start(f32[256,8,128]{2,1,0:T(8,128)} %whiten_pack.1) | copy-start | bytes 3145732

commit v4 on v3

--- a/solution.py
+++ b/solution.py
@@ -7,6 +7,9 @@
 from jax.experimental import pallas as pl
 from jax.experimental.pallas import tpu as pltpu
 from jax.sharding import PartitionSpec as P
+
+SUB = 16
+
 
 def whiten_kernel(ids_ref, counts_ref, x_ref, out_ref, used_ref):
     first = pl.program_id(0) == 0
@@ -22,48 +25,63 @@
             return c
         lax.fori_loop(0, homes, clear, 0)
 
-    x = x_ref[...]
-    x = jnp.concatenate([x[:, :128].reshape(group * 128, 128), x[:, 128:].reshape(group * 16, 128)], axis=0)
-    xf = x.astype(jnp.float32)
-    energy = xf * xf
-    high = energy.astype(jnp.bfloat16)
-    low = (energy - high.astype(jnp.float32)).astype(jnp.bfloat16)
     q = lax.broadcasted_iota(jnp.int32, (8, 128), 0)
     lane = lax.broadcasted_iota(jnp.int32, (8, 128), 1)
     start = (q // 2) * 16
     inside = (q < 6) & ((lane & 63) >= start) & ((lane & 63) < start + 32)
     window = jnp.where(inside, 1.0, 0.0).astype(jnp.bfloat16)
     center = jnp.where((q < 6) & (lane == start + 16 + (q & 1) * 64), 1.0, 0.0).astype(jnp.bfloat16)
+    none = jnp.zeros_like(window)
+    select = jnp.concatenate([jnp.concatenate([window, none], axis=1), jnp.concatenate([none, center], axis=1)], axis=0)
     contract = (((1,), (1,)), ((), ()))
-    total = lax.dot_general(jnp.concatenate([window, window], axis=1), jnp.concatenate([high, low], axis=1),
-                            contract, preferred_element_type=jnp.float32)
-    values = lax.dot_general(center, x, contract, preferred_element_type=jnp.float32)
-    white = values * lax.rsqrt(jnp.maximum(total * (1.0 / 32), 0.25))
-
     sub = lax.broadcasted_iota(jnp.int32, (8, 128), 0)
     chunk = lax.broadcasted_iota(jnp.int32, (8, 128), 1) // 16
-    for part in reversed(range(group // 8)):
-        base = group * 128 + part * 128
-        tail = white[:, base:base + 128]
-        turned = jnp.zeros_like(tail)
-        for d in range(8):
-            piece = jnp.where(((chunk - sub) & 7) == d, tail, 0.0)
-            if d:
-                piece = pltpu.roll(pltpu.roll(piece, 128 - 16 * d, 1), d, 0)
-            turned = turned + piece
-        for k in reversed(range(8)):
-            j = part * 8 + k
-            slot = step * group + j
-            station = ids_ref[slot]
-            home = (station * 43691) >> 22
-            live = slot < counts_ref[0]
-            seen = used_ref[home]
-            used_ref[home] = jnp.where(live, seen + 1, seen)
-            place = jnp.where(live, seen * homes + home, 0)
-            mark = (station - home * 96 + 1).astype(jnp.float32)
-            tile = jnp.where(sub < 6, white[:, j * 128:(j + 1) * 128],
-                             jnp.where(sub == 6, jnp.broadcast_to(turned[k:k + 1], (8, 128)), mark))
-            out_ref[place] = jnp.where(live, tile, 0.0)
+    def whitened(part):
+        x = x_ref[part * SUB:(part + 1) * SUB]
+        x = jnp.concatenate([x[:, :128].reshape(SUB * 128, 128), x[:, 128:].reshape(SUB * 16, 128)], axis=0)
+        xf = x.astype(jnp.float32)
+        energy = xf * xf
+        energy = energy + pltpu.roll(energy, 64, 1)
+        high = energy.astype(jnp.bfloat16).astype(jnp.float32)
+        left = lax.broadcasted_iota(jnp.int32, energy.shape, 1) < 64
+        mixed = jnp.where(left, high, energy - high).astype(jnp.bfloat16)
+        both = lax.dot_general(select, jnp.concatenate([mixed, x], axis=1), contract,
+                               preferred_element_type=jnp.float32)
+        total, values = both[:8], both[8:]
+        return values * lax.rsqrt(jnp.maximum(total * (1.0 / 32), 0.25))
+
+    def pack(part, white):
+        for eight in reversed(range(SUB // 8)):
+            base = SUB * 128 + eight * 128
+            tail = white[:, base:base + 128]
+            turned = jnp.zeros_like(tail)
+            for d in range(8):
+                piece = jnp.where(((chunk - sub) & 7) == d, tail, 0.0)
+                if d:
+                    piece = pltpu.roll(pltpu.roll(piece, 128 - 16 * d, 1), d, 0)
+                turned = turned + piece
+            for k in reversed(range(8)):
+                j = eight * 8 + k
+                slot = step * group + part * SUB + j
+                station = ids_ref[slot]
+                home = (station * 43691) >> 22
+                live = slot < counts_ref[0]
+                seen = used_ref[home]
+                used_ref[home] = jnp.where(live, seen + 1, seen)
+                place = jnp.where(live, seen * homes + home, 0)
+                mark = (station - home * 96 + 1).astype(jnp.float32)
+                tile = jnp.where(sub < 6, white[:, j * 128:(j + 1) * 128],
+                                 jnp.where(sub == 6, jnp.broadcast_to(turned[k:k + 1], (8, 128)), mark))
+                out_ref[place] = jnp.where(live, tile, 0.0)
+
+    parts = list(reversed(range(group // SUB)))
+    waiting = whitened(parts[0])
+    for part, following in zip(parts, parts[1:] + [None]):
+        ready = waiting
+        if following is not None:
+            waiting = whitened(following)
+        pack(part, ready)
+
 
 def whiten_pack(spectra, ids, counts, homes, group=8):
     slots, segs, width = spectra.shape
@@ -75,7 +93,7 @@
                   pl.BlockSpec((group, segs, width), lambda i: (slots // group - 1 - i, 0, 0))],
         out_specs=pl.BlockSpec((2 * homes, 8, 128), lambda i: (0, 0, 0)),
         scratch_shapes=[pltpu.SMEM((homes,), jnp.int32)],
-        compiler_params=pltpu.CompilerParams(vmem_limit_bytes=60 * 2**20),
+        compiler_params=pltpu.CompilerParams(vmem_limit_bytes=50 * 2**20),
         name="whiten_pack",
     )(ids, counts, spectra)
 
@@ -454,6 +472,7 @@
     readers = row_count * column_count
     slots, segments, _ = spectra.shape
     home_rows = slots // 2
+    station_ids = pltpu.with_memory_space_constraint(station_ids, pltpu.HBM)
     packed = whiten_pack(spectra, station_ids, counts, readers, group=48)
     packed = packed.reshape(2, RING, 2, RING, 2, 2, 8, 128)
     norm = 1.0 / math.sqrt(segments)

time: 74 us -> 70.2 us (0.949)
  Pallas kernels: 71.8 us -> 69.3 us
  local copies, waits for them, and re-layouts: 1.22 us -> 0 us
    pallas_call x1, Pallas kernels: 10.4 us -> 7.82 us  [whiten_pack(): pl.pallas_call(whiten_kernel, out_shape=jax.ShapeDtypeStruct((2 * homes,...]
    unnamed x2 -> x0, local copies, waits for them, and re-layouts: 1.22 us -> none
where the time goes in v4:
time: 70.2 us; the launch traced here: 70 us
  Pallas kernels  69.3 us (99%)
    pallas_call x1, Pallas kernels, exchange(): pl.pallas_call(functools.partial(exchange_kernel, norm), out_shape=(jax.S...  55.2 us
    pallas_call x1, Pallas kernels, whiten_pack(): pl.pallas_call(whiten_kernel, out_shape=jax.ShapeDtypeStruct((2 * homes,...  7.82 us
    pallas_call x1, Pallas kernels, finish(): pl.pallas_call(functools.partial(finish_kernel, norm), out_shape=jax.Shap...  6.38 us

profile of v4, /device:TPU:1, one launch (start us, length us, event | category | flops | bytes accessed | tf_op | source)
XLA Modules:
  0.0 70.0 jit_solution(4662108427239157388)
XLA Ops:
  0.7 7.8 %whiten_pack.1 = f32[256,8,128]{2,1,0:T(8,128)S(1)} custom-call(s32[192]{0:T(256)} %ids_ref.1, s32[1]{0:T(128)S(6)} %copy.4.counts_ref, bf16[192,144,128]{2,1,0:T(8,128)(2,1)} %x_ref.1), custom_call_target="tpu_custom_call" | custom-call | tf_op jit(solution)/shard_map/whiten_pack/pallas_call | solution.py:88
  8.5 55.2 %exchange.1 = (bf16[2,16,96,896]{3,2,1,0:T(8,128)(2,1)S(1)}, bf16[3,1536,896]{2,1,0:T(8,128)(2,1)S(1)}, bf16[13,3,2,96,768]{4,3,2,1,0:T(8,128)(2,1)S(1)}) custom-call(f32[2,4,2,4,2,2,8,128]{7,6,5,4,3,2,1,0:T(8,128)S(1)} %bitcast.1), custom_call_target="tpu_custom_call" | custom-call | tf_op jit(solution)/shard_map/exchange/pallas_call | solution.py:369
  63.6 6.4 %finish.1 = bf16[3,2,1536,768]{3,2,1,0:T(8,128)(2,1)} custom-call(bf16[2,16,96,896]{3,2,1,0:T(8,128)(2,1)S(1)} %get-tuple-element.8.rows_ref, bf16[3,1536,896]{2,1,0:T(8,128)(2,1)S(1)} %get-tuple-element.9.rhs_ref, bf16[13,3,2,96,768]{4,3,2,1,0:T(8,128)(2,1)S(1)} %get-tuple-element.10.part_ref), custom_call_target="tpu_custom_call" | custom-call | tf_op jit(solution)/shard_map/finish/pallas_call | solution.py:458
